TPU v7x, 256 devices: a whole 4x4x8 slice. The times are simulated.
256 devices in a mesh: ctx: 64 (over z, x_lo, y), kv: 4 (over x_hi, core).
Axes of the slice: x: 4 (x_hi: 2, x_lo: 2; x = x_hi * 2 + x_lo), y: 4, z: 8, core: 2. Of those that a mesh axis runs over, the one named last changes fastest.
Arguments:
- queries: float32 [2, 4096, 16384], P(None, 'ctx', 'kv'), may hold values from -5 to 5
- keys: float32 [2, 4096, 1024], P(None, 'ctx', 'kv'), may hold values from -5 to 5
- values: float32 [2, 4096, 1024], P(None, 'ctx', 'kv'), may hold values from -6 to 6
- query_maps: float32 [128, 128, 128], P('kv'), may hold values from -2.5 to 2.5
- key_maps: float32 [8, 128, 128], P('kv'), may hold values from -2.5 to 2.5
- mix: float32 [128], P('kv'), may hold values from -2 to 2
- window_blocks: int32 [2, 64], P(None, 'ctx'), may hold values from 0 to 255
- starts: int32 [2], replicated, may hold values from 0 to 1024, as said below
Outputs:
- attended: float32 [2, 4096, 16384], P(None, ('ctx', 'kv'))
Inputs may be any that keep to these rules, and one draw needn't show every extreme that they name: Every start lies between 0 and 1024; some sequence starts exactly at 1024.
All inputs are finite; a program needn't handle non-finite values.
Results may differ from a plain program's by a relative error of at most 0.0003.
Values sent between devices are 32-bit elements; how exact they have to be, the bound alone decides.
A program may use at most 128 MiB of HBM per device.

v0:
```python
import functools

import jax
import jax.numpy as jnp
from jax import lax
from jax.experimental import pallas as pl
from jax.experimental.pallas import tpu as pltpu
from jax.sharding import Mesh
from jax.sharding import PartitionSpec as P

HD = 128
HALF = 128
FEAT = 2 * HALF
BLOCK = 64
WBLK = 8
GROUP = 16
PLANE = 8
PLANES = 8
SEQS = 2
KVL = 2
COMBOS = SEQS * KVL
QL = KVL * GROUP * HD
WIN = 640
PIECE = 24
HEADS = 4
ROWS = BLOCK // 4
NEG = -1e30
CTX = ("ctx_0", "ctx_1", "ctx_2")
KV = ("kv_0", "kv_1")
CTX_KV = CTX + KV
MESH = pl.DeviceIdType.MESH
F32 = jnp.float32
BF16 = jnp.bfloat16
HIGHEST = lax.Precision.HIGHEST

NN = (((1,), (0,)), ((), ()))
NT = (((1,), (1,)), ((), ()))
TN = (((0,), (0,)), ((), ()))


def remote(src, dst, send, recv, device):
    return pltpu.make_async_remote_copy(
        src_ref=src, dst_ref=dst, send_sem=send, recv_sem=recv, device_id=device, device_id_type=MESH
    )


def mm(a, b, dims):
    return lax.dot_general(a, b, dims, preferred_element_type=F32)


def split(x):
    hi = x.astype(BF16)
    return hi, (x - hi.astype(F32)).astype(BF16)


def softmax_pair(logits):
    up = jnp.exp(logits)
    down = jnp.exp(-logits)
    up = up / jnp.sum(up, axis=-1, keepdims=True)
    down = down / jnp.sum(down, axis=-1, keepdims=True)
    return jnp.concatenate([up, down], axis=-1)


def here():
    return [lax.axis_index(a) for a in CTX_KV]


def features(x, weights):
    x_hi, x_lo = split(x)
    w_hi, w_lo = split(weights)
    w = jnp.concatenate([w_hi, w_lo], axis=1)
    both = mm(jnp.concatenate([x_hi, x_lo], axis=1), jnp.concatenate([w, w], axis=0), NN)
    return both[:, :HALF] + both[:, HALF:]


def kernel(
    starts_ref, bits_ref, mix_ref, q_hbm, k_hbm, v_hbm, qm_hbm, km_hbm, out,
    q, qm, km, own, prev, kvw, a_tx, a_rx, t_tx, t_rx, d_tx, far, p_hi, p_lo, near, mine,
    k_hi, k_lo, v_hi, v_lo, f_hi, f_lo,
    ld_own, ld_q, ld_qm, ld_km, z_send, z_recv, w_send, w_recv,
    a_send, a_recv, t_send, t_recv, d_send, d_recv, o_send, o_recv, o_own,
):
    z, x, y, h, c = here()
    me = x * 4 + y
    kv = h * 2 + c
    anchor = (z * PLANE + me) * BLOCK

    def lanes(n):
        return slice((n % KVL) * HD, (n % KVL + 1) * HD)

    def plane(o):
        j = lax.rem(me + o, PLANE)
        return j, (z, j // 4, lax.rem(j, 4), h, c)

    def column(o):
        j = lax.rem(z + o, PLANES)
        return j, (j, x, y, h, c)

    def line(o):
        j = lax.rem(y + o, 4)
        return j, (z, x, j, h, c)

    def ring(o):
        j = lax.rem(kv + o, 4)
        return j, (z, x, y, j // 2, lax.rem(j, 2))

    partner = (z, 1 - x, y, h, c)

    loads_own = {}
    for n in range(COMBOS):
        for t, hbm in enumerate((k_hbm, v_hbm)):
            loads_own[n, t] = pltpu.make_async_copy(hbm.at[n // KVL, :, lanes(n)], own.at[n, t], ld_own.at[n, t])
            loads_own[n, t].start()
    load_km = pltpu.make_async_copy(km_hbm, km, ld_km.at[0])
    load_km.start()
    loads_qm = []
    loads_q = []
    for g in range(KVL):
        loads_qm.append(
            pltpu.make_async_copy(qm_hbm.at[g * GROUP:(g + 1) * GROUP], qm.at[g * GROUP:(g + 1) * GROUP], ld_qm.at[g])
        )
    for n in range(COMBOS):
        g = n % KVL
        loads_q.append(
            pltpu.make_async_copy(q_hbm.at[n // KVL, :, g * GROUP * HD:(g + 1) * GROUP * HD], q.at[n], ld_q.at[n])
        )
    for copy in (loads_q[0], loads_qm[0], loads_q[1], loads_qm[1], loads_q[2], loads_q[3]):
        copy.start()

    barrier = pltpu.get_barrier_semaphore()
    greeted = [plane(o)[1] for o in range(1, PLANE)] + [column(o)[1] for o in range(1, PLANES)]
    greeted += [ring(o)[1] for o in range(1, 4)]
    for device in greeted:
        pl.semaphore_signal(barrier, inc=1, device_id=device, device_id_type=MESH)
    pl.semaphore_wait(barrier, len(greeted))

    def shift(n):
        return remote(own.at[n], prev.at[n], z_send.at[n], z_recv.at[n], column(1)[1])

    def to_line(n, o, source):
        return remote(source.at[n], kvw.at[n, me], w_send.at[n, o], w_recv.at[n, me], line(o)[1])

    def to_partner(n, source):
        return remote(source.at[n], kvw.at[n, me], w_send.at[n, 0], w_recv.at[n, me], partner)

    other = (1 - x) * 4 + y

    def forward(n, o):
        return remote(kvw.at[n, other], kvw.at[n, other], w_send.at[n, 3 + o], w_recv.at[n, other], line(o)[1])

    def window_own(n):
        @pl.when(x == 0)
        def _():
            to_partner(n, own).start()

        for o in range(1, 4):
            @pl.when(y + o < 4)
            def _():
                to_line(n, o, own).start()

    def window_prev(n):
        @pl.when(x == 1)
        def _():
            to_partner(n, prev).start()

        for o in range(1, 4):
            @pl.when(y + o >= 4)
            def _():
                to_line(n, o, prev).start()

        kvw[n, me] = prev[n]

    def arrived(n, slot):
        return remote(kvw.at[n, slot], kvw.at[n, slot], w_send.at[n, 0], w_recv.at[n, slot], partner)

    def window_forward(n):
        arrived(n, other).wait_recv()
        for o in range(1, 4):
            forward(n, o).start()

    def to_owner(n, o):
        j, device = plane(o)
        return remote(a_tx.at[n, j], a_rx.at[n, me], a_send.at[n, o], a_recv.at[n, me], device)

    def state(n):
        s, g = n // KVL, n % KVL
        shift(n).wait_recv()
        phi = softmax_pair(features(prev[n, 0], km[g]))
        row = lax.broadcasted_iota(jnp.int32, (BLOCK, FEAT), 0)
        position = row + (anchor - PLANE * BLOCK)
        phi = jnp.where((position >= 0) & (position >= starts_ref[s]), phi, 0.0)
        hi, lo = split(phi)
        v_h, v_l = split(prev[n, 1])
        total = mm(jnp.concatenate([v_h, v_l], axis=0), jnp.concatenate([hi, hi], axis=0), TN) + mm(v_h, lo, TN)
        norm = jnp.broadcast_to(jnp.sum(phi, axis=0, keepdims=True), (8, FEAT))
        for j in range(PLANE):
            a_tx[n, j, 0:16, :] = total[j * 16:(j + 1) * 16]
            a_tx[n, j, 16:24, :] = norm
        for o in range(1, PLANE):
            to_owner(n, o).start()
        a_rx[n, me] = a_tx[n, me]

    def from_plane(n, o, buf, send, recv):
        j = lax.rem(me - o + PLANE, PLANE)
        return remote(buf.at[n, j], buf.at[n, j], send.at[n, o], recv.at[n, j], plane(o)[1])

    def to_later(n, o):
        return remote(t_tx.at[n], t_rx.at[n, z], t_send.at[n, o], t_recv.at[n, z], column(o)[1])

    def owner_total(n):
        for o in range(1, PLANE):
            from_plane(n, o, a_rx, a_send, a_recv).wait_recv()
        total = a_rx[n, 0]
        for j in range(1, PLANE):
            total = total + a_rx[n, j]
        t_tx[n] = total
        for o in range(1, PLANES):
            @pl.when(z + o < PLANES)
            def _():
                to_later(n, o).start()

    def to_reader(n, o):
        j, device = plane(o)
        return remote(d_tx.at[n, j], far.at[n, me], d_send.at[n, o], d_recv.at[n, me], device)

    def owner_prefix(n):
        d_tx[n, 0] = jnp.zeros((PIECE, FEAT), F32)
        for j in range(PLANES - 1):
            @pl.when(j < z)
            def _():
                remote(t_tx.at[n], t_rx.at[n, j], t_send.at[n, 1], t_recv.at[n, j], partner).wait_recv()
                d_tx[n, 0] = d_tx[n, 0] + t_rx[n, j]
        running = d_tx[n, 0]
        for j in range(PLANE - 1):
            running = running + a_rx[n, j]
            d_tx[n, j + 1] = running
        for o in range(1, PLANE):
            to_reader(n, o).start()
        far[n, me] = d_tx[n, me]

    def query_features(n):
        g = n % KVL
        loads_q[n].wait()
        if n < KVL:
            loads_qm[g].wait()

        @pl.loop(0, GROUP // HEADS)
        def _(step):
            wide = q[n, :, pl.ds(pl.multiple_of(step * HEADS * HD, HEADS * HD), HEADS * HD)]
            logits = []
            for k in range(HEADS):
                logits.append(features(wide[:, k * HD:(k + 1) * HD], qm[g * GROUP + step * HEADS + k]))
            hi, lo = split(softmax_pair(jnp.concatenate(logits, axis=0)))
            place = pl.ds(pl.multiple_of(step * HEADS * BLOCK, HEADS * BLOCK), HEADS * BLOCK)
            p_hi[n, place, :] = hi
            p_lo[n, place, :] = lo

    def attend_near(n):
        s = n // KVL
        for o in range(1, 4):
            j = line(o)[0]
            arrived(n, x * 4 + j).wait_recv()
            arrived(n, (1 - x) * 4 + j).wait_recv()
        zeros = jnp.zeros((WIN - (WBLK + 1) * BLOCK, HD), F32)
        hi, lo = split(jnp.concatenate([kvw[n, j, 0] for j in range(PLANE)] + [own[n, 0], zeros], axis=0))
        k_hi[...] = jnp.concatenate([hi, hi], axis=1)
        k_lo[...] = jnp.concatenate([lo, lo], axis=1)
        hi, lo = split(jnp.concatenate([kvw[n, j, 1] for j in range(PLANE)] + [own[n, 1], zeros], axis=0))
        v_hi[...] = jnp.concatenate([hi, jnp.ones((WIN, HD), BF16)], axis=1)
        v_lo[...] = lo
        start = starts_ref[s]
        column_id = lax.broadcasted_iota(jnp.int32, (8, WIN), 1)
        slot = column_id // BLOCK
        distance = jnp.where(slot < me, me - slot, me - slot + PLANE)
        bits = jnp.broadcast_to(bits_ref[s, 0], (8, WIN))
        picked = lax.shift_right_logical(bits, jnp.maximum(distance - 1, 0)) & 1
        position = anchor - distance * BLOCK + (column_id & (BLOCK - 1))
        earlier = (slot < PLANE) & (picked == 1) & (position >= 0) & (position >= start)
        bias = jnp.where(earlier, 0.0, NEG)[:1, :WBLK * BLOCK]
        row = lax.broadcasted_iota(jnp.int32, (HEADS * BLOCK, HD), 0) & (BLOCK - 1)
        col = lax.broadcasted_iota(jnp.int32, (HEADS * BLOCK, HD), 1)
        own_bias = jnp.where((col <= row) & (anchor + col >= start), 0.0, NEG)

        @pl.loop(0, GROUP // HEADS)
        def _(step):
            wide = q[n, :, pl.ds(pl.multiple_of(step * HEADS * HD, HEADS * HD), HEADS * HD)]
            rows = jnp.concatenate([wide[:, k * HD:(k + 1) * HD] for k in range(HEADS)], axis=0)
            q_hi, q_lo = split(rows * HD ** -0.5)
            both = jnp.concatenate([q_hi, q_lo], axis=1)
            scores = mm(both, k_hi[...], NT) + mm(both, k_lo[...], NT)
            scores = jnp.concatenate(
                [scores[:, :WBLK * BLOCK] + bias, scores[:, WBLK * BLOCK:] + own_bias], axis=1
            )
            top = jnp.max(scores, axis=1, keepdims=True)
            e_hi, e_lo = split(jnp.exp(scores - top))
            wide_sum = mm(e_hi, v_hi[...], NN) + mm(e_lo, v_hi[...], NN)
            extra = mm(e_hi, v_lo[...], NN)
            place = pl.ds(pl.multiple_of(step * HEADS * BLOCK, HEADS * BLOCK), HEADS * BLOCK)
            near[n, place, :] = jnp.concatenate([wide_sum[:, :HD] + extra, wide_sum[:, HD:]], axis=1)

    def to_keeper(n, o):
        s, g = n // KVL, n % KVL
        j, device = ring(o)
        piece = mine.at[n, pl.ds(pl.multiple_of(j * ROWS, ROWS), ROWS), :]
        return remote(piece, out.at[s, :, columns(g, kv)], o_send.at[n, o], o_recv.at[n, kv], device)

    def columns(g, j):
        return pl.ds(pl.multiple_of(j * QL + g * GROUP * HD, GROUP * HD), GROUP * HD)

    def to_self(n):
        s, g = n // KVL, n % KVL
        piece = mine.at[n, pl.ds(pl.multiple_of(kv * ROWS, ROWS), ROWS), :]
        return pltpu.make_async_copy(piece, out.at[s, :, columns(g, kv)], o_own.at[n])

    def finish(n):
        s, g = n // KVL, n % KVL
        for o in range(1, PLANE):
            from_plane(n, o, far, d_send, d_recv).wait_recv()
        total = jnp.concatenate([far[n, j, 0:16, :] for j in range(PLANE)], axis=0)
        norm = jnp.broadcast_to(far[n, 0, 16:17, :], (HD, FEAT))
        hi, lo = split(jnp.concatenate([total, norm], axis=0))
        f_hi[...] = hi
        f_lo[...] = lo
        row = lax.broadcasted_iota(jnp.int32, (BLOCK, HD), 0)
        live = (row + anchor) >= starts_ref[s]

        @pl.loop(0, GROUP // HEADS)
        def _(step):
            place = pl.ds(pl.multiple_of(step * HEADS * BLOCK, HEADS * BLOCK), HEADS * BLOCK)
            hi = p_hi[n, place, :]
            distant = mm(hi, f_hi[...], NT) + mm(p_lo[n, place, :], f_hi[...], NT) + mm(hi, f_lo[...], NT)
            close = near[n, place, :]
            for k in range(HEADS):
                head = step * HEADS + k
                a = jax.nn.sigmoid(jnp.full((1, HD), mix_ref[g * GROUP + head], F32))
                part = slice(k * BLOCK, (k + 1) * BLOCK)
                top_part = a * close[part, :HD] + (1.0 - a) * distant[part, :HD]
                bottom = a * close[part, HD:] + (1.0 - a) * distant[part, HD:]
                result = jnp.where(live, top_part / jnp.where(live, bottom, 1.0), 0.0)
                mine[n, :, pl.ds(pl.multiple_of(head * HD, HD), HD)] = result

        for o in (2, 1, 3):
            to_keeper(n, o).start()
        to_self(n).start()

    for n in range(COMBOS):
        for t in range(2):
            loads_own[n, t].wait()
        shift(n).start()
    window_own(0)
    load_km.wait()
    query_features(0)
    for n in range(COMBOS):
        state(n)
        window_prev(n)
        if n + 1 < COMBOS:
            window_own(n + 1)
        if n > 0:
            window_forward(n - 1)
    owner_total(0)
    window_forward(COMBOS - 1)
    for n in range(1, COMBOS):
        query_features(n)
        owner_total(n)
    attend_near(0)
    owner_prefix(0)
    owner_prefix(1)
    attend_near(1)
    owner_prefix(2)
    owner_prefix(3)
    finish(0)
    attend_near(2)
    finish(1)
    attend_near(3)
    finish(2)
    finish(3)

    for n in range(COMBOS):
        shift(n).wait_send()
        to_partner(n, own).wait_send()
        for o in range(1, 4):
            to_line(n, o, own).wait_send()
            forward(n, o).wait_send()
        for o in range(1, PLANE):
            to_owner(n, o).wait_send()
            to_reader(n, o).wait_send()
        for o in range(1, PLANES):
            @pl.when(z + o < PLANES)
            def _():
                to_later(n, o).wait_send()
    for n in range(COMBOS):
        s, g = n // KVL, n % KVL
        to_self(n).wait()
        for o in range(1, 4):
            to_keeper(n, o).wait_send()
            j = lax.rem(kv - o + 4, 4)
            landed = out.at[s, :, columns(g, j)]
            remote(landed, landed, o_send.at[n, o], o_recv.at[n, j], ring(o)[1]).wait_recv()


def on_device(queries, keys, values, query_maps, key_maps, mix, window_blocks, starts):
    smem = pl.BlockSpec(memory_space=pltpu.SMEM)
    hbm = pl.BlockSpec(memory_space=pl.ANY)
    dma = pltpu.SemaphoreType.DMA
    vmem = pltpu.VMEM
    pieces = (COMBOS, PLANE, PIECE, FEAT)
    return pl.pallas_call(
        kernel,
        out_shape=jax.ShapeDtypeStruct((SEQS, ROWS, 4 * QL), F32),
        in_specs=[smem, smem, smem] + [hbm] * 5,
        out_specs=hbm,
        scratch_shapes=[
            vmem((COMBOS, BLOCK, GROUP * HD), F32),
            vmem((KVL * GROUP, HD, HALF), F32),
            vmem((KVL, HD, HALF), F32),
            vmem((COMBOS, 2, BLOCK, HD), F32),
            vmem((COMBOS, 2, BLOCK, HD), F32),
            vmem((COMBOS, PLANE, 2, BLOCK, HD), F32),
            vmem(pieces, F32),
            vmem(pieces, F32),
            vmem((COMBOS, PIECE, FEAT), F32),
            vmem(pieces, F32),
            vmem(pieces, F32),
            vmem(pieces, F32),
            vmem((COMBOS, GROUP * BLOCK, FEAT), BF16),
            vmem((COMBOS, GROUP * BLOCK, FEAT), BF16),
            vmem((COMBOS, GROUP * BLOCK, 2 * HD), F32),
            vmem((COMBOS, BLOCK, GROUP * HD), F32),
            vmem((WIN, 2 * HD), BF16),
            vmem((WIN, 2 * HD), BF16),
            vmem((WIN, 2 * HD), BF16),
            vmem((WIN, HD), BF16),
            vmem((2 * HD, FEAT), BF16),
            vmem((2 * HD, FEAT), BF16),
            dma((COMBOS, 2)), dma((COMBOS,)), dma((KVL,)), dma((1,)), dma((COMBOS,)), dma((COMBOS,)),
            dma((COMBOS, 7)), dma((COMBOS, 8)),
            dma((COMBOS, 8)), dma((COMBOS, 8)), dma((COMBOS, 8)), dma((COMBOS, 8)), dma((COMBOS, 8)), dma((COMBOS, 8)),
            dma((COMBOS, 4)), dma((COMBOS, 4)), dma((COMBOS,)),
        ],
        name="hybrid",
        compiler_params=pltpu.CompilerParams(
            collective_id=0, has_side_effects=True, vmem_limit_bytes=62 << 20
        ),
    )(starts, window_blocks, mix, queries, keys, values, query_maps, key_maps)


def solution(mesh):
    torus = Mesh(mesh.devices.reshape(8, 2, 4, 2, 2), ("ctx_0", "ctx_1", "ctx_2", "kv_0", "kv_1"))
    in_specs = (
        P(None, CTX, KV),
        P(None, CTX, KV),
        P(None, CTX, KV),
        P(KV, None, None),
        P(KV, None, None),
        P(KV),
        P(None, CTX),
        P(),
    )
    out_specs = P(None, CTX_KV, None)
    return jax.shard_map(
        on_device, mesh=torus, in_specs=in_specs, out_specs=out_specs, check_vma=False
    )
```

profile of v0, /device:TPU:1, one launch (start us, length us, event | category | flops | bytes accessed | tf_op | source)
XLA Modules:
  0.0 84.5 jit_solution(11571625416861660605)
XLA Ops:
  0.0 1.3 %copy.9.bits_ref = s32[2,1]{1,0:T(2,128)} copy(s32[2,1]{0,1:T(1,128)} %param.14) | data formatting | bytes 16 | tf_op args[6]
  1.3 80.1 %hybrid.1 = f32[2,16,16384]{2,1,0:T(8,128)} custom-call(s32[2]{0:T(128)} %starts_ref.1, s32[2,1]{1,0:T(2,128)} %copy.9.bits_ref, f32[32]{0:T(128)} %mix_ref.1, f32[2,64,4096]{2,1,0:T(8,128)} %q_hbm.1, f32[2,64,256]{2,1,0:T(8,128)} %k_hbm.1, f32[2,64,256]{2,1,0:T(8,128)} %v_hbm.1, f32[32,128,128]{2,1,0:T(8,128)} %qm_hbm.1, f32[2,128,128]{2,1,0:T(8,128)} %km_hbm.1), custom_call_target="tpu_custom_call" | custom-call | tf_op jit(solution)/shard_map/hybrid/pallas_call | solution.py:407
  81.4 3.0 %copy.11 = f32[2,16,16384]{2,1,0:T(8,128)} copy(f32[2,16,16384]{2,1,0:T(8,128)} %hybrid.1) | data formatting | bytes 4194304
where the time goes:
time: 84.9 us; the launch traced here: 84.5 us
  Pallas kernels  80.1 us (94%)
  local copies, waits for them, and re-layouts  4.34 us (5%)
    pallas_call x1, Pallas kernels, on_device(): pl.pallas_call(kernel, out_shape=jax.ShapeDtypeStruct((SEQS, ROWS, 4 * QL...  80.1 us
    unnamed x2, local copies, waits for them, and re-layouts  4.34 us

commit v1 on v0

--- a/solution.py
+++ b/solution.py
@@ -21,8 +21,9 @@
 COMBOS = SEQS * KVL
 QL = KVL * GROUP * HD
 WIN = 640
-PIECE = 24
+PIECE = 16
 HEADS = 4
+STEPS = GROUP // HEADS
 ROWS = BLOCK // 4
 NEG = -1e30
 CTX = ("ctx_0", "ctx_1", "ctx_2")
@@ -76,9 +77,10 @@
 def kernel(
     starts_ref, bits_ref, mix_ref, q_hbm, k_hbm, v_hbm, qm_hbm, km_hbm, out,
     q, qm, km, own, prev, kvw, a_tx, a_rx, t_tx, t_rx, d_tx, far, p_hi, p_lo, near, mine,
-    k_hi, k_lo, v_hi, v_lo, f_hi, f_lo,
+    k_hi, k_lo, v_hi, v_lo, f_hi, f_lo, n_tx, n_rx, m_tx, m_rx, norms,
     ld_own, ld_q, ld_qm, ld_km, z_send, z_recv, w_send, w_recv,
     a_send, a_recv, t_send, t_recv, d_send, d_recv, o_send, o_recv, o_own,
+    n_send, n_recv, m_send, m_recv,
 ):
     z, x, y, h, c = here()
     me = x * 4 + y
@@ -153,7 +155,7 @@
         def _():
             to_partner(n, own).start()
 
-        for o in range(1, 4):
+        for o in (1, 3):
             @pl.when(y + o < 4)
             def _():
                 to_line(n, o, own).start()
@@ -163,7 +165,7 @@
         def _():
             to_partner(n, prev).start()
 
-        for o in range(1, 4):
+        for o in (1, 3):
             @pl.when(y + o >= 4)
             def _():
                 to_line(n, o, prev).start()
@@ -175,8 +177,27 @@
 
     def window_forward(n):
         arrived(n, other).wait_recv()
-        for o in range(1, 4):
+        for o in (1, 3):
             forward(n, o).start()
+
+    swing = 1 - 2 * lax.rem(y, 2)
+    ahead = lax.rem(y + swing + 4, 4)
+    behind = lax.rem(y - swing + 4, 4)
+
+    def relay(n, slot, k, to):
+        return remote(kvw.at[n, slot], kvw.at[n, slot], w_send.at[n, k], w_recv.at[n, slot], (z, x, to, h, c))
+
+    def relay_same(n):
+        return relay(n, x * 4 + behind, 2, ahead)
+
+    def relay_other(n):
+        return relay(n, (1 - x) * 4 + ahead, 5, behind)
+
+    def window_relay(n):
+        arrived(n, x * 4 + behind).wait_recv()
+        relay_same(n).start()
+        arrived(n, (1 - x) * 4 + ahead).wait_recv()
+        relay_other(n).start()
 
     def to_owner(n, o):
         j, device = plane(o)
@@ -192,13 +213,46 @@
         hi, lo = split(phi)
         v_h, v_l = split(prev[n, 1])
         total = mm(jnp.concatenate([v_h, v_l], axis=0), jnp.concatenate([hi, hi], axis=0), TN) + mm(v_h, lo, TN)
-        norm = jnp.broadcast_to(jnp.sum(phi, axis=0, keepdims=True), (8, FEAT))
         for j in range(PLANE):
-            a_tx[n, j, 0:16, :] = total[j * 16:(j + 1) * 16]
-            a_tx[n, j, 16:24, :] = norm
+            a_tx[n, j] = total[j * PIECE:(j + 1) * PIECE]
+        n_tx[n:n + 1, :] = jnp.sum(phi, axis=0, keepdims=True)
         for o in range(1, PLANE):
             to_owner(n, o).start()
         a_rx[n, me] = a_tx[n, me]
+
+    def norm_to_plane(o):
+        return remote(n_tx, n_rx.at[me], n_send.at[o], n_recv.at[me], plane(o)[1])
+
+    def norm_to_later(o):
+        return remote(m_tx, m_rx.at[z], m_send.at[o], m_recv.at[z], column(o)[1])
+
+    def norm_start():
+        for o in range(1, PLANE):
+            norm_to_plane(o).start()
+        n_rx[me] = n_tx[...]
+
+    def norm_total():
+        for o in range(1, PLANE):
+            j = lax.rem(me - o + PLANE, PLANE)
+            remote(n_rx.at[j], n_rx.at[j], n_send.at[o], n_recv.at[j], plane(o)[1]).wait_recv()
+        total = jnp.zeros((8, FEAT), F32)
+        inside = jnp.zeros((8, FEAT), F32)
+        for j in range(PLANE):
+            total = total + n_rx[j]
+            inside = jnp.where(j < me, total, inside)
+        m_tx[...] = total
+        norms[...] = inside
+        for o in range(1, PLANES):
+            @pl.when(z + o < PLANES)
+            def _():
+                norm_to_later(o).start()
+
+    def norm_finish():
+        for j in range(PLANES - 1):
+            @pl.when(j < z)
+            def _():
+                remote(m_tx, m_rx.at[j], m_send.at[1], m_recv.at[j], partner).wait_recv()
+                norms[...] = norms[...] + m_rx[j]
 
     def from_plane(n, o, buf, send, recv):
         j = lax.rem(me - o + PLANE, PLANE)
@@ -244,7 +298,7 @@
         if n < KVL:
             loads_qm[g].wait()
 
-        @pl.loop(0, GROUP // HEADS)
+        @pl.loop(0, STEPS)
         def _(step):
             wide = q[n, :, pl.ds(pl.multiple_of(step * HEADS * HD, HEADS * HD), HEADS * HD)]
             logits = []
@@ -257,10 +311,9 @@
 
     def attend_near(n):
         s = n // KVL
-        for o in range(1, 4):
-            j = line(o)[0]
-            arrived(n, x * 4 + j).wait_recv()
-            arrived(n, (1 - x) * 4 + j).wait_recv()
+        opposite = line(2)[0]
+        for slot in (x * 4 + ahead, x * 4 + opposite, (1 - x) * 4 + behind, (1 - x) * 4 + opposite):
+            arrived(n, slot).wait_recv()
         zeros = jnp.zeros((WIN - (WBLK + 1) * BLOCK, HD), F32)
         hi, lo = split(jnp.concatenate([kvw[n, j, 0] for j in range(PLANE)] + [own[n, 0], zeros], axis=0))
         k_hi[...] = jnp.concatenate([hi, hi], axis=1)
@@ -272,7 +325,7 @@
         column_id = lax.broadcasted_iota(jnp.int32, (8, WIN), 1)
         slot = column_id // BLOCK
         distance = jnp.where(slot < me, me - slot, me - slot + PLANE)
-        bits = jnp.broadcast_to(bits_ref[s, 0], (8, WIN))
+        bits = jnp.broadcast_to(bits_ref[0, s], (8, WIN))
         picked = lax.shift_right_logical(bits, jnp.maximum(distance - 1, 0)) & 1
         position = anchor - distance * BLOCK + (column_id & (BLOCK - 1))
         earlier = (slot < PLANE) & (picked == 1) & (position >= 0) & (position >= start)
@@ -281,7 +334,7 @@
         col = lax.broadcasted_iota(jnp.int32, (HEADS * BLOCK, HD), 1)
         own_bias = jnp.where((col <= row) & (anchor + col >= start), 0.0, NEG)
 
-        @pl.loop(0, GROUP // HEADS)
+        @pl.loop(0, STEPS)
         def _(step):
             wide = q[n, :, pl.ds(pl.multiple_of(step * HEADS * HD, HEADS * HD), HEADS * HD)]
             rows = jnp.concatenate([wide[:, k * HD:(k + 1) * HD] for k in range(HEADS)], axis=0)
@@ -298,33 +351,44 @@
             place = pl.ds(pl.multiple_of(step * HEADS * BLOCK, HEADS * BLOCK), HEADS * BLOCK)
             near[n, place, :] = jnp.concatenate([wide_sum[:, :HD] + extra, wide_sum[:, HD:]], axis=1)
 
-    def to_keeper(n, o):
+    def landing(n, step, j):
         s, g = n // KVL, n % KVL
+        width = HEADS * HD
+        return out.at[s, :, pl.ds(pl.multiple_of(j * QL + g * GROUP * HD + step * width, width), width)]
+
+    def piece(n, step, j):
+        width = HEADS * HD
+        return mine.at[
+            n, pl.ds(pl.multiple_of(j * ROWS, ROWS), ROWS), pl.ds(pl.multiple_of(step * width, width), width)
+        ]
+
+    def to_keeper(n, step, o):
         j, device = ring(o)
-        piece = mine.at[n, pl.ds(pl.multiple_of(j * ROWS, ROWS), ROWS), :]
-        return remote(piece, out.at[s, :, columns(g, kv)], o_send.at[n, o], o_recv.at[n, kv], device)
-
-    def columns(g, j):
-        return pl.ds(pl.multiple_of(j * QL + g * GROUP * HD, GROUP * HD), GROUP * HD)
-
-    def to_self(n):
-        s, g = n // KVL, n % KVL
-        piece = mine.at[n, pl.ds(pl.multiple_of(kv * ROWS, ROWS), ROWS), :]
-        return pltpu.make_async_copy(piece, out.at[s, :, columns(g, kv)], o_own.at[n])
+        return remote(
+            piece(n, step, j), landing(n, step, kv), o_send.at[n, o, step], o_recv.at[n, kv, step], device
+        )
+
+    def to_self(n, step):
+        return pltpu.make_async_copy(piece(n, step, kv), landing(n, step, kv), o_own.at[n, step])
+
+    def from_ring(n, step, o):
+        j = lax.rem(kv - o + 4, 4)
+        landed = landing(n, step, j)
+        return remote(landed, landed, o_send.at[n, o, step], o_recv.at[n, j, step], ring(o)[1])
 
     def finish(n):
         s, g = n // KVL, n % KVL
         for o in range(1, PLANE):
             from_plane(n, o, far, d_send, d_recv).wait_recv()
-        total = jnp.concatenate([far[n, j, 0:16, :] for j in range(PLANE)], axis=0)
-        norm = jnp.broadcast_to(far[n, 0, 16:17, :], (HD, FEAT))
+        total = jnp.concatenate([far[n, j] for j in range(PLANE)], axis=0)
+        norm = jnp.broadcast_to(norms[n:n + 1, :], (HD, FEAT))
         hi, lo = split(jnp.concatenate([total, norm], axis=0))
         f_hi[...] = hi
         f_lo[...] = lo
         row = lax.broadcasted_iota(jnp.int32, (BLOCK, HD), 0)
         live = (row + anchor) >= starts_ref[s]
 
-        @pl.loop(0, GROUP // HEADS)
+        @pl.loop(0, STEPS)
         def _(step):
             place = pl.ds(pl.multiple_of(step * HEADS * BLOCK, HEADS * BLOCK), HEADS * BLOCK)
             hi = p_hi[n, place, :]
@@ -338,10 +402,9 @@
                 bottom = a * close[part, HD:] + (1.0 - a) * distant[part, HD:]
                 result = jnp.where(live, top_part / jnp.where(live, bottom, 1.0), 0.0)
                 mine[n, :, pl.ds(pl.multiple_of(head * HD, HD), HD)] = result
-
-        for o in (2, 1, 3):
-            to_keeper(n, o).start()
-        to_self(n).start()
+            for o in (2, 1, 3):
+                to_keeper(n, step, o).start()
+            to_self(n, step).start()
 
     for n in range(COMBOS):
         for t in range(2):
@@ -349,38 +412,58 @@
         shift(n).start()
     window_own(0)
     load_km.wait()
+    n_tx[...] = jnp.zeros((8, FEAT), F32)
     query_features(0)
-    for n in range(COMBOS):
-        state(n)
-        window_prev(n)
-        if n + 1 < COMBOS:
-            window_own(n + 1)
-        if n > 0:
-            window_forward(n - 1)
+    state(0)
+    window_prev(0)
+    window_own(1)
+    state(1)
+    window_prev(1)
+    window_forward(0)
+    window_own(2)
+    state(2)
+    window_prev(2)
+    window_forward(1)
+    window_relay(0)
+    window_own(3)
+    state(3)
+    norm_start()
+    window_prev(3)
+    window_forward(2)
+    window_relay(1)
     owner_total(0)
-    window_forward(COMBOS - 1)
-    for n in range(1, COMBOS):
-        query_features(n)
-        owner_total(n)
+    window_forward(3)
+    window_relay(2)
+    query_features(1)
+    owner_total(1)
+    window_relay(3)
+    query_features(2)
+    owner_total(2)
+    norm_total()
+    query_features(3)
+    owner_total(3)
+    owner_prefix(0)
     attend_near(0)
-    owner_prefix(0)
     owner_prefix(1)
+    norm_finish()
+    finish(0)
     attend_near(1)
     owner_prefix(2)
+    finish(1)
+    attend_near(2)
     owner_prefix(3)
-    finish(0)
-    attend_near(2)
-    finish(1)
+    finish(2)
     attend_near(3)
-    finish(2)
     finish(3)
 
     for n in range(COMBOS):
         shift(n).wait_send()
         to_partner(n, own).wait_send()
-        for o in range(1, 4):
+        for o in (1, 3):
             to_line(n, o, own).wait_send()
             forward(n, o).wait_send()
+        relay_same(n).wait_send()
+        relay_other(n).wait_send()
         for o in range(1, PLANE):
             to_owner(n, o).wait_send()
             to_reader(n, o).wait_send()
@@ -388,19 +471,24 @@
             @pl.when(z + o < PLANES)
             def _():
                 to_later(n, o).wait_send()
+    for o in range(1, PLANE):
+        norm_to_plane(o).wait_send()
+    for o in range(1, PLANES):
+        @pl.when(z + o < PLANES)
+        def _():
+            norm_to_later(o).wait_send()
     for n in range(COMBOS):
-        s, g = n // KVL, n % KVL
-        to_self(n).wait()
-        for o in range(1, 4):
-            to_keeper(n, o).wait_send()
-            j = lax.rem(kv - o + 4, 4)
-            landed = out.at[s, :, columns(g, j)]
-            remote(landed, landed, o_send.at[n, o], o_recv.at[n, j], ring(o)[1]).wait_recv()
+        @pl.loop(0, STEPS)
+        def _(step):
+            to_self(n, step).wait()
+            for o in range(1, 4):
+                to_keeper(n, step, o).wait_send()
+                from_ring(n, step, o).wait_recv()
 
 
 def on_device(queries, keys, values, query_maps, key_maps, mix, window_blocks, starts):
     smem = pl.BlockSpec(memory_space=pltpu.SMEM)
-    hbm = pl.BlockSpec(memory_space=pl.ANY)
+    hbm = pl.BlockSpec(memory_space=pltpu.HBM)
     dma = pltpu.SemaphoreType.DMA
     vmem = pltpu.VMEM
     pieces = (COMBOS, PLANE, PIECE, FEAT)
@@ -408,7 +496,7 @@
         kernel,
         out_shape=jax.ShapeDtypeStruct((SEQS, ROWS, 4 * QL), F32),
         in_specs=[smem, smem, smem] + [hbm] * 5,
-        out_specs=hbm,
+        out_specs=pl.BlockSpec(memory_space=pl.ANY),
         scratch_shapes=[
             vmem((COMBOS, BLOCK, GROUP * HD), F32),
             vmem((KVL * GROUP, HD, HALF), F32),
@@ -432,16 +520,22 @@
             vmem((WIN, HD), BF16),
             vmem((2 * HD, FEAT), BF16),
             vmem((2 * HD, FEAT), BF16),
+            vmem((8, FEAT), F32),
+            vmem((PLANE, 8, FEAT), F32),
+            vmem((8, FEAT), F32),
+            vmem((PLANES, 8, FEAT), F32),
+            vmem((8, FEAT), F32),
             dma((COMBOS, 2)), dma((COMBOS,)), dma((KVL,)), dma((1,)), dma((COMBOS,)), dma((COMBOS,)),
             dma((COMBOS, 7)), dma((COMBOS, 8)),
             dma((COMBOS, 8)), dma((COMBOS, 8)), dma((COMBOS, 8)), dma((COMBOS, 8)), dma((COMBOS, 8)), dma((COMBOS, 8)),
-            dma((COMBOS, 4)), dma((COMBOS, 4)), dma((COMBOS,)),
+            dma((COMBOS, 4, STEPS)), dma((COMBOS, 4, STEPS)), dma((COMBOS, STEPS)),
+            dma((8,)), dma((8,)), dma((8,)), dma((8,)),
         ],
         name="hybrid",
         compiler_params=pltpu.CompilerParams(
-            collective_id=0, has_side_effects=True, vmem_limit_bytes=62 << 20
+            collective_id=0, has_side_effects=True, vmem_limit_bytes=61 << 20
         ),
-    )(starts, window_blocks, mix, queries, keys, values, query_maps, key_maps)
+    )(starts, window_blocks.T, mix, queries, keys, values, query_maps, key_maps)
 
 
 def solution(mesh):

time: 84.9 us -> 78.8 us (0.928)
  Pallas kernels: 80.1 us -> 75.7 us
  local copies, waits for them, and re-layouts: 4.34 us -> 3.05 us
    pallas_call x1, Pallas kernels: 80.1 us -> 75.7 us  [on_device(): pl.pallas_call(kernel, out_shape=jax.ShapeDtypeStruct((SEQS, ROWS, 4 * QL...]
    unnamed x2 -> x1, local copies, waits for them, and re-layouts: 4.34 us -> 3.05 us
where the time goes in v1:
time: 78.8 us; the launch traced here: 78.7 us
  Pallas kernels  75.7 us (96%)
  local copies, waits for them, and re-layouts  3.05 us (4%)
    pallas_call x1, Pallas kernels, on_device(): pl.pallas_call(kernel, out_shape=jax.ShapeDtypeStruct((SEQS, ROWS, 4 * QL...  75.7 us
    unnamed x1, local copies, waits for them, and re-layouts  3.05 us

profile of v1, /device:TPU:1, one launch (start us, length us, event | category | flops | bytes accessed | tf_op | source)
XLA Modules:
  0.0 78.7 jit_solution(14125628152899920315)
XLA Ops:
  0.0 75.7 %hybrid.1 = f32[2,16,16384]{2,1,0:T(8,128)} custom-call(s32[2]{0:T(128)} %starts_ref.1, s32[1,2]{1,0:T(1,128)} %bitcast.1, f32[32]{0:T(128)} %mix_ref.1, f32[2,64,4096]{2,1,0:T(8,128)} %q_hbm.1, f32[2,64,256]{2,1,0:T(8,128)} %k_hbm.1, f32[2,64,256]{2,1,0:T(8,128)} %v_hbm.1, f32[32,128,128]{2,1,0:T(8,128)} %qm_hbm.1, f32[2,128,128]{2,1,0:T(8,128)} %km_hbm.1), custom_call_target="tpu_custom_call" | custom-call | tf_op jit(solution)/shard_map/hybrid/pallas_call | solution.py:495
  75.7 3.0 %copy.10 = f32[2,16,16384]{2,1,0:T(8,128)} copy(f32[2,16,16384]{2,1,0:T(8,128)} %hybrid.1) | data formatting | bytes 4194304

commit v2 on v1

--- a/solution.py
+++ b/solution.py
@@ -22,7 +22,7 @@
 QL = KVL * GROUP * HD
 WIN = 640
 PIECE = 16
-HEADS = 4
+HEADS = 8
 STEPS = GROUP // HEADS
 ROWS = BLOCK // 4
 NEG = -1e30
@@ -77,7 +77,7 @@
 def kernel(
     starts_ref, bits_ref, mix_ref, q_hbm, k_hbm, v_hbm, qm_hbm, km_hbm, out,
     q, qm, km, own, prev, kvw, a_tx, a_rx, t_tx, t_rx, d_tx, far, p_hi, p_lo, near, mine,
-    k_hi, k_lo, v_hi, v_lo, f_hi, f_lo, n_tx, n_rx, m_tx, m_rx, norms,
+    k_hi, k_lo, v_both, f_both, n_tx, n_rx, m_tx, m_rx, norms,
     ld_own, ld_q, ld_qm, ld_km, z_send, z_recv, w_send, w_recv,
     a_send, a_recv, t_send, t_recv, d_send, d_recv, o_send, o_recv, o_own,
     n_send, n_recv, m_send, m_recv,
@@ -126,7 +126,7 @@
         loads_q.append(
             pltpu.make_async_copy(q_hbm.at[n // KVL, :, g * GROUP * HD:(g + 1) * GROUP * HD], q.at[n], ld_q.at[n])
         )
-    for copy in (loads_q[0], loads_qm[0], loads_q[1], loads_qm[1], loads_q[2], loads_q[3]):
+    for copy in (loads_q[0], loads_q[2], loads_qm[0], loads_q[1], loads_q[3], loads_qm[1]):
         copy.start()
 
     barrier = pltpu.get_barrier_semaphore()
@@ -292,22 +292,25 @@
             to_reader(n, o).start()
         far[n, me] = d_tx[n, me]
 
-    def query_features(n):
-        g = n % KVL
-        loads_q[n].wait()
-        if n < KVL:
-            loads_qm[g].wait()
-
-        @pl.loop(0, STEPS)
+    def query_features(g):
+        for n in (g, g + KVL):
+            loads_q[n].wait()
+        loads_qm[g].wait()
+
+        @pl.loop(0, GROUP // 4)
         def _(step):
-            wide = q[n, :, pl.ds(pl.multiple_of(step * HEADS * HD, HEADS * HD), HEADS * HD)]
+            span = pl.ds(pl.multiple_of(step * 4 * HD, 4 * HD), 4 * HD)
+            wide = jnp.concatenate([q[g, :, span], q[g + KVL, :, span]], axis=0)
             logits = []
-            for k in range(HEADS):
-                logits.append(features(wide[:, k * HD:(k + 1) * HD], qm[g * GROUP + step * HEADS + k]))
+            for k in range(4):
+                logits.append(features(wide[:, k * HD:(k + 1) * HD], qm[g * GROUP + step * 4 + k]))
             hi, lo = split(softmax_pair(jnp.concatenate(logits, axis=0)))
-            place = pl.ds(pl.multiple_of(step * HEADS * BLOCK, HEADS * BLOCK), HEADS * BLOCK)
-            p_hi[n, place, :] = hi
-            p_lo[n, place, :] = lo
+            for t in range(SEQS):
+                for k in range(4):
+                    place = pl.ds(pl.multiple_of((step * 4 + k) * BLOCK, BLOCK), BLOCK)
+                    part = slice((k * SEQS + t) * BLOCK, (k * SEQS + t + 1) * BLOCK)
+                    p_hi[t * KVL + g, place, :] = hi[part]
+                    p_lo[t * KVL + g, place, :] = lo[part]
 
     def attend_near(n):
         s = n // KVL
@@ -319,8 +322,7 @@
         k_hi[...] = jnp.concatenate([hi, hi], axis=1)
         k_lo[...] = jnp.concatenate([lo, lo], axis=1)
         hi, lo = split(jnp.concatenate([kvw[n, j, 1] for j in range(PLANE)] + [own[n, 1], zeros], axis=0))
-        v_hi[...] = jnp.concatenate([hi, jnp.ones((WIN, HD), BF16)], axis=1)
-        v_lo[...] = lo
+        v_both[...] = jnp.concatenate([hi, lo], axis=1)
         start = starts_ref[s]
         column_id = lax.broadcasted_iota(jnp.int32, (8, WIN), 1)
         slot = column_id // BLOCK
@@ -345,11 +347,13 @@
                 [scores[:, :WBLK * BLOCK] + bias, scores[:, WBLK * BLOCK:] + own_bias], axis=1
             )
             top = jnp.max(scores, axis=1, keepdims=True)
-            e_hi, e_lo = split(jnp.exp(scores - top))
-            wide_sum = mm(e_hi, v_hi[...], NN) + mm(e_lo, v_hi[...], NN)
-            extra = mm(e_hi, v_lo[...], NN)
+            weights = jnp.exp(scores - top)
+            e_hi, e_lo = split(weights)
+            both = mm(e_hi, v_both[...], NN)
+            close = both[:, :HD] + both[:, HD:] + mm(e_lo, v_both[:, :HD], NN)
+            mass = jnp.broadcast_to(jnp.sum(weights, axis=1, keepdims=True), close.shape)
             place = pl.ds(pl.multiple_of(step * HEADS * BLOCK, HEADS * BLOCK), HEADS * BLOCK)
-            near[n, place, :] = jnp.concatenate([wide_sum[:, :HD] + extra, wide_sum[:, HD:]], axis=1)
+            near[n, place, :] = jnp.concatenate([close, mass], axis=1)
 
     def landing(n, step, j):
         s, g = n // KVL, n % KVL
@@ -381,10 +385,9 @@
         for o in range(1, PLANE):
             from_plane(n, o, far, d_send, d_recv).wait_recv()
         total = jnp.concatenate([far[n, j] for j in range(PLANE)], axis=0)
-        norm = jnp.broadcast_to(norms[n:n + 1, :], (HD, FEAT))
-        hi, lo = split(jnp.concatenate([total, norm], axis=0))
-        f_hi[...] = hi
-        f_lo[...] = lo
+        hi, lo = split(total)
+        f_both[...] = jnp.concatenate([hi, lo], axis=0)
+        norm = norms[n:n + 1, :]
         row = lax.broadcasted_iota(jnp.int32, (BLOCK, HD), 0)
         live = (row + anchor) >= starts_ref[s]
 
@@ -392,14 +395,19 @@
         def _(step):
             place = pl.ds(pl.multiple_of(step * HEADS * BLOCK, HEADS * BLOCK), HEADS * BLOCK)
             hi = p_hi[n, place, :]
-            distant = mm(hi, f_hi[...], NT) + mm(p_lo[n, place, :], f_hi[...], NT) + mm(hi, f_lo[...], NT)
+            lo = p_lo[n, place, :]
+            both = mm(hi, f_both[...], NT)
+            distant = both[:, :HD] + both[:, HD:] + mm(lo, f_both[:HD, :], NT)
+            seen = (hi.astype(F32) + lo.astype(F32)) * norm
+            seen = jnp.sum(seen[:, :HALF] + seen[:, HALF:], axis=1, keepdims=True)
+            seen = jnp.broadcast_to(seen, distant.shape)
             close = near[n, place, :]
             for k in range(HEADS):
                 head = step * HEADS + k
                 a = jax.nn.sigmoid(jnp.full((1, HD), mix_ref[g * GROUP + head], F32))
                 part = slice(k * BLOCK, (k + 1) * BLOCK)
                 top_part = a * close[part, :HD] + (1.0 - a) * distant[part, :HD]
-                bottom = a * close[part, HD:] + (1.0 - a) * distant[part, HD:]
+                bottom = a * close[part, HD:] + (1.0 - a) * seen[part]
                 result = jnp.where(live, top_part / jnp.where(live, bottom, 1.0), 0.0)
                 mine[n, :, pl.ds(pl.multiple_of(head * HD, HD), HD)] = result
             for o in (2, 1, 3):
@@ -410,48 +418,46 @@
         for t in range(2):
             loads_own[n, t].wait()
         shift(n).start()
-    window_own(0)
     load_km.wait()
     n_tx[...] = jnp.zeros((8, FEAT), F32)
+    window_own(0)
     query_features(0)
     state(0)
     window_prev(0)
     window_own(1)
     state(1)
-    window_prev(1)
+    state(2)
     window_forward(0)
-    window_own(2)
-    state(2)
-    window_prev(2)
-    window_forward(1)
-    window_relay(0)
-    window_own(3)
     state(3)
     norm_start()
+    owner_total(0)
+    window_prev(1)
+    window_relay(0)
+    owner_total(1)
+    window_own(2)
+    owner_total(2)
+    window_forward(1)
+    owner_total(3)
+    window_prev(2)
+    norm_total()
+    query_features(1)
+    window_relay(1)
+    owner_prefix(0)
+    window_forward(2)
+    window_own(3)
     window_prev(3)
-    window_forward(2)
-    window_relay(1)
-    owner_total(0)
-    window_forward(3)
-    window_relay(2)
-    query_features(1)
-    owner_total(1)
-    window_relay(3)
-    query_features(2)
-    owner_total(2)
-    norm_total()
-    query_features(3)
-    owner_total(3)
-    owner_prefix(0)
     attend_near(0)
     owner_prefix(1)
     norm_finish()
     finish(0)
+    window_relay(2)
+    owner_prefix(2)
     attend_near(1)
-    owner_prefix(2)
     finish(1)
+    window_forward(3)
+    owner_prefix(3)
+    window_relay(3)
     attend_near(2)
-    owner_prefix(3)
     finish(2)
     attend_near(3)
     finish(3)
@@ -517,8 +523,6 @@
             vmem((WIN, 2 * HD), BF16),
             vmem((WIN, 2 * HD), BF16),
             vmem((WIN, 2 * HD), BF16),
-            vmem((WIN, HD), BF16),
-            vmem((2 * HD, FEAT), BF16),
             vmem((2 * HD, FEAT), BF16),
             vmem((8, FEAT), F32),
             vmem((PLANE, 8, FEAT), F32),

time: 78.8 us -> 68.3 us (0.87)
  Pallas kernels: 75.7 us -> 65.2 us
    pallas_call x1, Pallas kernels: 75.7 us -> 65.2 us  [on_device(): pl.pallas_call(kernel, out_shape=jax.ShapeDtypeStruct((SEQS, ROWS, 4 * QL...]
where the time goes in v2:
time: 68.3 us; the launch traced here: 68.2 us
  Pallas kernels  65.2 us (95%)
  local copies, waits for them, and re-layouts  3.05 us (4%)
    pallas_call x1, Pallas kernels, on_device(): pl.pallas_call(kernel, out_shape=jax.ShapeDtypeStruct((SEQS, ROWS, 4 * QL...  65.2 us
    unnamed x1, local copies, waits for them, and re-layouts  3.05 us

profile of v2, /device:TPU:1, one launch (start us, length us, event | category | flops | bytes accessed | tf_op | source)
XLA Modules:
  0.0 68.2 jit_solution(17622136876784163662)
XLA Ops:
  0.0 65.2 %hybrid.1 = f32[2,16,16384]{2,1,0:T(8,128)} custom-call(s32[2]{0:T(128)} %starts_ref.1, s32[1,2]{1,0:T(1,128)} %bitcast.1, f32[32]{0:T(128)} %mix_ref.1, f32[2,64,4096]{2,1,0:T(8,128)} %q_hbm.1, f32[2,64,256]{2,1,0:T(8,128)} %k_hbm.1, f32[2,64,256]{2,1,0:T(8,128)} %v_hbm.1, f32[32,128,128]{2,1,0:T(8,128)} %qm_hbm.1, f32[2,128,128]{2,1,0:T(8,128)} %km_hbm.1), custom_call_target="tpu_custom_call" | custom-call | tf_op jit(solution)/shard_map/hybrid/pallas_call | solution.py:501
  65.2 3.0 %copy.10 = f32[2,16,16384]{2,1,0:T(8,128)} copy(f32[2,16,16384]{2,1,0:T(8,128)} %hybrid.1) | data formatting | bytes 4194304

commit v3 on v2

--- a/solution.py
+++ b/solution.py
@@ -108,6 +108,12 @@
 
     partner = (z, 1 - x, y, h, c)
 
+    barrier = pltpu.get_barrier_semaphore()
+    greeted = [plane(o)[1] for o in range(1, PLANE)] + [column(o)[1] for o in range(1, PLANES)]
+    greeted += [ring(o)[1] for o in range(1, 4)]
+    for device in greeted:
+        pl.semaphore_signal(barrier, inc=1, device_id=device, device_id_type=MESH)
+
     loads_own = {}
     for n in range(COMBOS):
         for t, hbm in enumerate((k_hbm, v_hbm)):
@@ -129,11 +135,6 @@
     for copy in (loads_q[0], loads_q[2], loads_qm[0], loads_q[1], loads_q[3], loads_qm[1]):
         copy.start()
 
-    barrier = pltpu.get_barrier_semaphore()
-    greeted = [plane(o)[1] for o in range(1, PLANE)] + [column(o)[1] for o in range(1, PLANES)]
-    greeted += [ring(o)[1] for o in range(1, 4)]
-    for device in greeted:
-        pl.semaphore_signal(barrier, inc=1, device_id=device, device_id_type=MESH)
     pl.semaphore_wait(barrier, len(greeted))
 
     def shift(n):
@@ -193,9 +194,11 @@
     def relay_other(n):
         return relay(n, (1 - x) * 4 + ahead, 5, behind)
 
-    def window_relay(n):
+    def window_relay_same(n):
         arrived(n, x * 4 + behind).wait_recv()
         relay_same(n).start()
+
+    def window_relay_other(n):
         arrived(n, (1 - x) * 4 + ahead).wait_recv()
         relay_other(n).start()
 
@@ -242,13 +245,13 @@
             inside = jnp.where(j < me, total, inside)
         m_tx[...] = total
         norms[...] = inside
-        for o in range(1, PLANES):
-            @pl.when(z + o < PLANES)
+        for o in range(1, PLANES - 1):
+            @pl.when((z > 0) & (z + o < PLANES))
             def _():
                 norm_to_later(o).start()
 
     def norm_finish():
-        for j in range(PLANES - 1):
+        for j in range(1, PLANES - 1):
             @pl.when(j < z)
             def _():
                 remote(m_tx, m_rx.at[j], m_send.at[1], m_recv.at[j], partner).wait_recv()
@@ -268,8 +271,8 @@
         for j in range(1, PLANE):
             total = total + a_rx[n, j]
         t_tx[n] = total
-        for o in range(1, PLANES):
-            @pl.when(z + o < PLANES)
+        for o in range(1, PLANES - 1):
+            @pl.when((z > 0) & (z + o < PLANES))
             def _():
                 to_later(n, o).start()
 
@@ -279,7 +282,7 @@
 
     def owner_prefix(n):
         d_tx[n, 0] = jnp.zeros((PIECE, FEAT), F32)
-        for j in range(PLANES - 1):
+        for j in range(1, PLANES - 1):
             @pl.when(j < z)
             def _():
                 remote(t_tx.at[n], t_rx.at[n, j], t_send.at[n, 1], t_recv.at[n, j], partner).wait_recv()
@@ -432,7 +435,8 @@
     norm_start()
     owner_total(0)
     window_prev(1)
-    window_relay(0)
+    window_relay_same(0)
+    window_relay_other(0)
     owner_total(1)
     window_own(2)
     owner_total(2)
@@ -441,22 +445,25 @@
     window_prev(2)
     norm_total()
     query_features(1)
-    window_relay(1)
+    window_relay_same(1)
+    window_relay_other(1)
     owner_prefix(0)
     window_forward(2)
     window_own(3)
     window_prev(3)
-    attend_near(0)
     owner_prefix(1)
     norm_finish()
+    attend_near(0)
+    owner_prefix(2)
     finish(0)
-    window_relay(2)
-    owner_prefix(2)
+    window_relay_same(2)
+    window_relay_other(2)
+    window_forward(3)
     attend_near(1)
+    owner_prefix(3)
     finish(1)
-    window_forward(3)
-    owner_prefix(3)
-    window_relay(3)
+    window_relay_same(3)
+    window_relay_other(3)
     attend_near(2)
     finish(2)
     attend_near(3)
@@ -473,14 +480,14 @@
         for o in range(1, PLANE):
             to_owner(n, o).wait_send()
             to_reader(n, o).wait_send()
-        for o in range(1, PLANES):
-            @pl.when(z + o < PLANES)
+        for o in range(1, PLANES - 1):
+            @pl.when((z > 0) & (z + o < PLANES))
             def _():
                 to_later(n, o).wait_send()
     for o in range(1, PLANE):
         norm_to_plane(o).wait_send()
-    for o in range(1, PLANES):
-        @pl.when(z + o < PLANES)
+    for o in range(1, PLANES - 1):
+        @pl.when((z > 0) & (z + o < PLANES))
         def _():
             norm_to_later(o).wait_send()
     for n in range(COMBOS):

time: 68.3 us -> 67.7 us (level)
  Pallas kernels: 65.2 us -> 64.5 us
where the time goes in v3:
time: 67.7 us; the launch traced here: 67.6 us
  Pallas kernels  64.5 us (95%)
  local copies, waits for them, and re-layouts  3.05 us (5%)
    pallas_call x1, Pallas kernels, on_device(): pl.pallas_call(kernel, out_shape=jax.ShapeDtypeStruct((SEQS, ROWS, 4 * QL...  64.5 us
    unnamed x1, local copies, waits for them, and re-layouts  3.05 us

profile of v3, /device:TPU:1, one launch (start us, length us, event | category | flops | bytes accessed | tf_op | source)
XLA Modules:
  0.0 67.6 jit_solution(15317913204424935120)
XLA Ops:
  0.0 64.5 %hybrid.1 = f32[2,16,16384]{2,1,0:T(8,128)} custom-call(s32[2]{0:T(128)} %starts_ref.1, s32[1,2]{1,0:T(1,128)} %bitcast.1, f32[32]{0:T(128)} %mix_ref.1, f32[2,64,4096]{2,1,0:T(8,128)} %q_hbm.1, f32[2,64,256]{2,1,0:T(8,128)} %k_hbm.1, f32[2,64,256]{2,1,0:T(8,128)} %v_hbm.1, f32[32,128,128]{2,1,0:T(8,128)} %qm_hbm.1, f32[2,128,128]{2,1,0:T(8,128)} %km_hbm.1), custom_call_target="tpu_custom_call" | custom-call | tf_op jit(solution)/shard_map/hybrid/pallas_call | solution.py:508
  64.5 3.0 %copy.10 = f32[2,16,16384]{2,1,0:T(8,128)} copy(f32[2,16,16384]{2,1,0:T(8,128)} %hybrid.1) | data formatting | bytes 4194304

commit v4 on v3

--- a/solution.py
+++ b/solution.py
@@ -22,7 +22,7 @@
 QL = KVL * GROUP * HD
 WIN = 640
 PIECE = 16
-HEADS = 8
+HEADS = 16
 STEPS = GROUP // HEADS
 ROWS = BLOCK // 4
 NEG = -1e30

time: 67.7 us -> 67.3 us (level)
  no operation moved by 1% of the time
where the time goes in v4:
time: 67.3 us; the launch traced here: 67.2 us
  Pallas kernels  64.1 us (95%)
  local copies, waits for them, and re-layouts  3.05 us (5%)
    pallas_call x1, Pallas kernels, on_device(): pl.pallas_call(kernel, out_shape=jax.ShapeDtypeStruct((SEQS, ROWS, 4 * QL...  64.1 us
    unnamed x1, local copies, waits for them, and re-layouts  3.05 us

profile of v4, /device:TPU:1, one launch (start us, length us, event | category | flops | bytes accessed | tf_op | source)
XLA Modules:
  0.0 67.2 jit_solution(9750995366675945526)
XLA Ops:
  0.0 64.1 %hybrid.1 = f32[2,16,16384]{2,1,0:T(8,128)} custom-call(s32[2]{0:T(128)} %starts_ref.1, s32[1,2]{1,0:T(1,128)} %bitcast.1, f32[32]{0:T(128)} %mix_ref.1, f32[2,64,4096]{2,1,0:T(8,128)} %q_hbm.1, f32[2,64,256]{2,1,0:T(8,128)} %k_hbm.1, f32[2,64,256]{2,1,0:T(8,128)} %v_hbm.1, f32[32,128,128]{2,1,0:T(8,128)} %qm_hbm.1, f32[2,128,128]{2,1,0:T(8,128)} %km_hbm.1), custom_call_target="tpu_custom_call" | custom-call | tf_op jit(solution)/shard_map/hybrid/pallas_call | solution.py:508
  64.1 3.0 %copy.10 = f32[2,16,16384]{2,1,0:T(8,128)} copy(f32[2,16,16384]{2,1,0:T(8,128)} %hybrid.1) | data formatting | bytes 4194304
